TPU v7x, 32 devices: a whole 2x2x4 slice. The times are simulated.
32 devices in a mesh: depth: 4 (over z), tile: 8 (over y, x, core).
Axes of the slice: x: 2, y: 2, z: 4, core: 2. Of those that a mesh axis runs over, the one named last changes fastest.
Arguments:
- density: bfloat16 [32, 256, 1024], P('depth', None, 'tile'), may hold values from 0 to 1
- view_zoom: float32 [2], replicated, may hold values from 0.5 to 0.9
- view_shift: float32 [2], replicated, may hold values from 0 to 16
- tf_weights: float32 [2, 4, 8], replicated, may hold values from 0.25 to 2
- perm_order: int32 [2, 4], replicated, may hold values from 0 to 3, each once within a row
Outputs:
- image: float32 [2, 4, 256, 1024], P(None, None, 'depth', 'tile')
All inputs are finite; a program needn't handle non-finite values.
Results may differ from a plain program's by a relative error of at most 0.0028.
Values may be sent and summed in bfloat16 or wider, within the bound.
A program may use at most 64 MiB of HBM per device.

v0:
```python
import jax
import jax.numpy as jnp
from jax import lax
from jax.sharding import PartitionSpec as P

RADIUS = 8
OCCLUSION_GAIN = 1.5
EXTINCTION = 0.5


def with_halo(block, sides, width):
    for axis, dim in sides:
        count = lax.axis_size(axis)
        forward = [(i, i + 1) for i in range(count - 1)]
        backward = [(target, source) for source, target in forward]
        low = lax.ppermute(
            lax.slice_in_dim(block, block.shape[dim] - width, None, axis=dim), axis, forward
        )
        high = lax.ppermute(lax.slice_in_dim(block, 0, width, axis=dim), axis, backward)
        block = jnp.concatenate([low, block, high], axis=dim)
    return block


def blur_weights(radius):
    offsets = jnp.arange(-radius, radius + 1, dtype=jnp.float32)
    tap_weights = jnp.exp(-offsets * offsets / 72.0)
    return tap_weights / jnp.sum(tap_weights)


def occlusion_of(padded, radius, depth_cells, width_cells):
    tap_weights = blur_weights(radius)
    tap_count = 2 * radius + 1
    row_count = padded.shape[1]
    along_depth = tap_weights[0] * padded[0:depth_cells].astype(jnp.float32)
    for tap_index in range(1, tap_count):
        along_depth = along_depth + tap_weights[tap_index] * padded[
            tap_index : tap_index + depth_cells
        ].astype(jnp.float32)
    padded_rows = jnp.pad(along_depth, ((0, 0), (radius, radius), (0, 0)))
    along_rows = tap_weights[0] * padded_rows[:, 0:row_count]
    for tap_index in range(1, tap_count):
        along_rows = (
            along_rows + tap_weights[tap_index] * padded_rows[:, tap_index : tap_index + row_count]
        )
    along_width = tap_weights[0] * along_rows[:, :, 0:width_cells]
    for tap_index in range(1, tap_count):
        along_width = (
            along_width
            + tap_weights[tap_index] * along_rows[:, :, tap_index : tap_index + width_cells]
        )
    return jnp.exp(-OCCLUSION_GAIN * along_width).astype(jnp.bfloat16)


def resample_table(view_zoom, view_shift, row_count):
    pixel_pos = jnp.arange(row_count, dtype=jnp.float32)
    where_at = view_zoom[:, None] * pixel_pos[None, :] + view_shift[:, None]
    cell_pos = jnp.arange(row_count, dtype=jnp.float32)
    interp_table = jnp.maximum(0.0, 1.0 - jnp.abs(where_at[:, :, None] - cell_pos[None, None, :]))
    return interp_table.reshape(-1, row_count).astype(jnp.bfloat16)


def render_slab(slab_density, slab_shade, interp_table, tf_weights, depth_total):
    view_count = tf_weights.shape[0]
    basis_count = tf_weights.shape[2]
    row_count = slab_density.shape[1]
    width_cells = slab_density.shape[2]

    def one_slice(state_pair, cell_pair):
        colour, passing = state_pair
        density_rows, shade_rows = cell_pair
        stacked = jnp.concatenate([density_rows, shade_rows], axis=1)
        sampled = jnp.dot(interp_table, stacked, preferred_element_type=jnp.float32)
        sampled = sampled.reshape(view_count, row_count, 2 * width_cells)
        sampled_density = sampled[:, :, :width_cells]
        sampled_shade = sampled[:, :, width_cells:]
        values = jnp.zeros((view_count, 4, row_count, width_cells), jnp.float32)
        for basis_index in range(basis_count):
            offset = sampled_density * (basis_count - 1) - basis_index
            bump_value = jnp.exp(-0.5 * offset * offset)
            values = values + tf_weights[:, :, basis_index][:, :, None, None] * bump_value[:, None]
        opacity = 1.0 - jnp.exp(-(EXTINCTION / depth_total) * values[:, 3])
        lit_part = sampled_shade * opacity
        emitted = jnp.concatenate([values[:, 0:3] * lit_part[:, None], opacity[:, None]], axis=1)
        colour = colour + passing[:, None] * emitted
        passing = passing * (1.0 - opacity)
        return ((colour, passing), None)

    initial = (
        jnp.zeros((view_count, 4, row_count, width_cells), jnp.float32),
        jnp.ones((view_count, row_count, width_cells), jnp.float32),
    )
    final_state, _ = lax.scan(one_slice, initial, (slab_density, slab_shade))
    return final_state[0].astype(jnp.bfloat16)


def local(density, view_zoom, view_shift, tf_weights, perm_order):
    depth_cells = density.shape[0]
    row_count = density.shape[1]
    width_cells = density.shape[2]
    slab_count = lax.axis_size("depth")
    depth_total = depth_cells * slab_count
    padded = with_halo(density, (("depth", 0), ("tile", 2)), RADIUS)
    shade = occlusion_of(padded, RADIUS, depth_cells, width_cells)
    interp_table = resample_table(view_zoom, view_shift, row_count)
    slab_rgba = render_slab(density, shade, interp_table, tf_weights, depth_total)
    slot_ids = jnp.arange(slab_count, dtype=jnp.int32)
    selector = (perm_order[:, :, None] == slot_ids[None, None, :]).astype(jnp.bfloat16)
    ordered = jnp.einsum(
        "vqj,jvcrx->vqcrx",
        selector,
        lax.all_to_all(slab_rgba[None], "depth", split_axis=3, concat_axis=0, tiled=True),
        preferred_element_type=jnp.float32,
    )
    running = jnp.cumprod(1.0 - ordered[:, :, 3], axis=1)
    leading_ones = jnp.ones_like(running[:, 0:1])
    ahead_pass = jnp.concatenate([leading_ones, running[:, :-1]], axis=1)
    return jnp.sum(ahead_pass[:, :, None] * ordered, axis=1)


def solution(mesh):
    placed = (P("depth", None, "tile"), P(), P(), P(), P())
    return jax.shard_map(
        local, mesh=mesh, in_specs=placed, out_specs=P(None, None, "depth", "tile"), check_vma=False
    )
```

profile of v0, /device:TPU:4, one launch (start us, length us, event | category | flops | bytes accessed | tf_op | source)
XLA Modules:
  0.0 164.9 jit_solution(16466884867182730106)
XLA Ops:
  0.0 1.2 copy.51
  1.3 3.5 %collective-permute-start = (bf16[8,256,128]{1,2,0:T(8,128)(2,1)S(1)}, bf16[8,256,128]{1,2,0:T(8,128)(2,1)S(1)}, u32[]{:S(2)}, u32[]{:S(2)}) collective-permute-start(bf16[8,256,128]{1,2,0:T(8,128)(2,1)S(1)} %copy.51), channel_id=1, source_target_pairs={{0,8},{8,16},{16,24},{1,9},{9,17},{17,25},{2,10},{10,18},{18,26},{... | collective-permute-start | bytes 1572872 | tf_op jit(solution)/shard_map/ppermute | solution.py:16
  4.8 1.3 collective-permute-start.1
  8.9 7.0 %collective-permute-done = bf16[8,256,128]{1,2,0:T(8,128)(2,1)S(1)} collective-permute-done((bf16[8,256,128]{1,2,0:T(8,128)(2,1)S(1)}, bf16[8,256,128]{1,2,0:T(8,128)(2,1)S(1)}, u32[]{:S(2)}, u32[]{:S(2)}) %collective-permute-start) | collective-permute-done | bytes 524320 | tf_op jit(solution)/shard_map/ppermute | solution.py:16
  15.9 4.1 %collective-permute-done.1 = bf16[8,256,128]{1,2,0:T(8,128)(2,1)S(1)} collective-permute-done((bf16[8,256,128]{1,2,0:T(8,128)(2,1)S(1)}, bf16[8,256,128]{1,2,0:T(8,128)(2,1)S(1)}, u32[]{:S(2)}, u32[]{:S(2)}) %collective-permute-start.1) | collective-permute-done | bytes 524320 | tf_op jit(solution)/shard_map/ppermute | solution.py:19
  20.1 1.9 %collective-permute-start.2 = (bf16[24,256,8]{1,2,0:T(8,128)(2,1)S(1)}, bf16[24,256,8]{1,2,0:T(8,128)(2,1)S(1)}, u32[]{:S(2)}, u32[]{:S(2)}) collective-permute-start(bf16[24,256,8]{1,2,0:T(8,128)(2,1)S(1)} %get-tuple-element.190), channel_id=1, source_target_pairs={{0,1},{1,2},{2,3},{3,4},{4,5},{5,6},{6,7},{8,9},{9,10},{10,11},{11... | collective-permute-start | bytes 294920 | tf_op jit(solution)/shard_map/ppermute | solution.py:16
  22.0 4.5 %collective-permute-start.3 = (bf16[24,256,8]{1,2,0:T(8,128)(2,1)S(1)}, bf16[24,256,8]{1,2,0:T(8,128)(2,1)S(1)}, u32[]{:S(2)}, u32[]{:S(2)}) collective-permute-start(bf16[24,256,8]{1,2,0:T(8,128)(2,1)S(1)} %get-tuple-element.191), channel_id=1, source_target_pairs={{1,0},{2,1},{3,2},{4,3},{5,4},{6,5},{7,6},{9,8},{10,9},{11,10},{12... | collective-permute-start | bytes 294920 | tf_op jit(solution)/shard_map/ppermute | solution.py:19
  27.3 1.5 collective-permute-done.3
  28.9 12.5 %multiply_add_fusion.1 = f32[8,256,144]{1,2,0:T(8,128)S(1)} fusion(bf16[24,256,144]{1,2,0:T(8,128)(2,1)S(1)} %pad_maximum_fusion, f32[]{:T(128)} %bitcast.18, f32[]{:T(128)} %bitcast.17, f32[]{:T(128)} %bitcast.16, f32[]{:T(128)} %bitcast.15, f32[]{:T(128)} %bitcast.14, f32[]{:T(128)} %bitcast.13, f32[]{:T(128)} %bitcast.12, f32[]{:T(128)} %bitcast.11, ...), kind=kLoop, calls=%fused_computation.98 | loop fusion | flops 14745600 | bytes 11206724 | tf_op jit(solution)/shard_map/add | solution.py:36
  41.4 15.6 %fusion.38 = f32[8,256,144]{1,2,0:T(8,128)S(1)} fusion(f32[8,256,144]{1,2,0:T(8,128)S(1)} %multiply_add_fusion.1, f32[]{:T(128)} %bitcast.18, f32[]{:T(128)} %bitcast.17, f32[]{:T(128)} %bitcast.16, f32[]{:T(128)} %bitcast.15, f32[]{:T(128)} %bitcast.14, f32[]{:T(128)} %bitcast.13, f32[]{:T(128)} %bitcast.12, f32[]{:T(128)} %bitcast.11, f32[]{:T(128)} %bitcast.10, ...), kind=kLoop, calls=%fused_computation.82 | loop fusion | flops 9732096 | bytes 2359364 | tf_op jit(solution)/shard_map/add | solution.py:43
  56.9 12.8 %fusion.57 = bf16[8,256,128]{1,2,0:T(8,128)(2,1)S(1)} fusion(f32[8,256,144]{1,2,0:T(8,128)S(1)} %fusion.38, f32[]{:T(128)} %bitcast.18, f32[]{:T(128)} %bitcast.17, f32[]{:T(128)} %bitcast.16, f32[]{:T(128)} %bitcast.15, f32[]{:T(128)} %bitcast.14, f32[]{:T(128)} %bitcast.13, f32[]{:T(128)} %bitcast.12, f32[]{:T(128)} %bitcast.11, f32[]{:T(128)} %bitcast.10, ...), kind=kLoop, calls=%fused_computation.103 | loop fusion | flops 9175040 | bytes 18350148 | tf_op jit(solution)/shard_map/convert_element_type | solution.py:51
  69.7 72.9 %while.15 = (s32[]{:T(128)}, f32[2,4,256,128]{3,2,0,1:T(8,128)S(1)}, f32[2,256,128]{2,1,0:T(8,128)}, f32[2,4,8]{1,0,2:T(2,128)S(1)}, bf16[8,256,128]{2,1,0:T(8,1...) while((s32[]{:T(128)}, ...), condition=%wide.region_2.3_spmd.clone, body=%wide.region_1.2_spmd.clone.sunk | while | flops 75300864 | bytes 19140008 | solution.py:92
  70.7 0.9 dynamic-slice_bitcast_fusion.2
  72.1 1.3 multiply_exponential_fusion.2
  74.1 1.9 %multiply_add_fusion.3 = f32[2,4,256,128]{3,2,0,1:T(8,128)S(1)} fusion(f32[2,256,128]{2,1,0:T(8,128)} %get-tuple-element.271, f32[2,4]{0,1:T(4,128)S(1)} %copy.83, f32[2,256,128]{2,1,0:T(8,128)} %get-tuple-element.273, f32[2,4]{0,1:T(4,128)S(1)} %copy.84, f32[2,256,128]{2,1,0:T(8,128)} %get-tuple-element.275, f32[2,4]{0,1:T(4,128)S(1)} %copy.85, ...), kind=kLoop, calls=%fused_computation.4.clone.1 | loop fusion | flops 3932160 | bytes 3145984 | tf_op jit(solution)/shard_map/while/body/eval_jaxpr/add | solution.py:80
  78.0 0.8 copy-done
  78.9 0.9 dynamic-slice_bitcast_fusion.2
  80.4 1.3 multiply_exponential_fusion.2
  82.4 1.9 %multiply_add_fusion.3 = f32[2,4,256,128]{3,2,0,1:T(8,128)S(1)} fusion(f32[2,256,128]{2,1,0:T(8,128)} %get-tuple-element.271, f32[2,4]{0,1:T(4,128)S(1)} %copy.83, f32[2,256,128]{2,1,0:T(8,128)} %get-tuple-element.273, f32[2,4]{0,1:T(4,128)S(1)} %copy.84, f32[2,256,128]{2,1,0:T(8,128)} %get-tuple-element.275, f32[2,4]{0,1:T(4,128)S(1)} %copy.85, ...), kind=kLoop, calls=%fused_computation.4.clone.1 | loop fusion | flops 3932160 | bytes 3145984 | tf_op jit(solution)/shard_map/while/body/eval_jaxpr/add | solution.py:80
  84.4 1.7 %fusion.90 = (f32[2,256,128]{2,1,0:T(8,128)}, f32[2,256,128]{2,1,0:T(8,128)S(1)}, f32[2,256,128]{2,1,0:T(8,128)S(1)}) fusion(f32[2,4,256,128]{3,2,0,1:T(8,128)S(1)} %multiply_add_fusion.3, f32[2,256,128]{2,1,0:T(8,128)} %get-tuple-element.301, pred[]{:T(512)S(6)} %compare.5, f32[2,256,256]{2,1,0:T(8,128)S(1)} %bitcast.77), kind=kLoop, calls=%fused_computation.26.clone.1 | loop fusion | flops 393216 | bytes 1572865 | tf_op jit(solution)/shard_map/while/body/eval_jaxpr/mul | solution.py:85
  87.3 0.8 copy-done
  88.2 0.9 dynamic-slice_bitcast_fusion.2
  89.6 1.3 multiply_exponential_fusion.2
  91.7 1.9 %multiply_add_fusion.3 = f32[2,4,256,128]{3,2,0,1:T(8,128)S(1)} fusion(f32[2,256,128]{2,1,0:T(8,128)} %get-tuple-element.271, f32[2,4]{0,1:T(4,128)S(1)} %copy.83, f32[2,256,128]{2,1,0:T(8,128)} %get-tuple-element.273, f32[2,4]{0,1:T(4,128)S(1)} %copy.84, f32[2,256,128]{2,1,0:T(8,128)} %get-tuple-element.275, f32[2,4]{0,1:T(4,128)S(1)} %copy.85, ...), kind=kLoop, calls=%fused_computation.4.clone.1 | loop fusion | flops 3932160 | bytes 3145984 | tf_op jit(solution)/shard_map/while/body/eval_jaxpr/add | solution.py:80
  93.6 1.7 %fusion.90 = (f32[2,256,128]{2,1,0:T(8,128)}, f32[2,256,128]{2,1,0:T(8,128)S(1)}, f32[2,256,128]{2,1,0:T(8,128)S(1)}) fusion(f32[2,4,256,128]{3,2,0,1:T(8,128)S(1)} %multiply_add_fusion.3, f32[2,256,128]{2,1,0:T(8,128)} %get-tuple-element.301, pred[]{:T(512)S(6)} %compare.5, f32[2,256,256]{2,1,0:T(8,128)S(1)} %bitcast.77), kind=kLoop, calls=%fused_computation.26.clone.1 | loop fusion | flops 393216 | bytes 1572865 | tf_op jit(solution)/shard_map/while/body/eval_jaxpr/mul | solution.py:85
  96.5 0.8 copy-done
  97.4 0.9 dynamic-slice_bitcast_fusion.2
  98.8 1.3 multiply_exponential_fusion.2
  100.9 1.9 %multiply_add_fusion.3 = f32[2,4,256,128]{3,2,0,1:T(8,128)S(1)} fusion(f32[2,256,128]{2,1,0:T(8,128)} %get-tuple-element.271, f32[2,4]{0,1:T(4,128)S(1)} %copy.83, f32[2,256,128]{2,1,0:T(8,128)} %get-tuple-element.273, f32[2,4]{0,1:T(4,128)S(1)} %copy.84, f32[2,256,128]{2,1,0:T(8,128)} %get-tuple-element.275, f32[2,4]{0,1:T(4,128)S(1)} %copy.85, ...), kind=kLoop, calls=%fused_computation.4.clone.1 | loop fusion | flops 3932160 | bytes 3145984 | tf_op jit(solution)/shard_map/while/body/eval_jaxpr/add | solution.py:80
  102.8 1.7 %fusion.90 = (f32[2,256,128]{2,1,0:T(8,128)}, f32[2,256,128]{2,1,0:T(8,128)S(1)}, f32[2,256,128]{2,1,0:T(8,128)S(1)}) fusion(f32[2,4,256,128]{3,2,0,1:T(8,128)S(1)} %multiply_add_fusion.3, f32[2,256,128]{2,1,0:T(8,128)} %get-tuple-element.301, pred[]{:T(512)S(6)} %compare.5, f32[2,256,256]{2,1,0:T(8,128)S(1)} %bitcast.77), kind=kLoop, calls=%fused_computation.26.clone.1 | loop fusion | flops 393216 | bytes 1572865 | tf_op jit(solution)/shard_map/while/body/eval_jaxpr/mul | solution.py:85
  106.6 0.9 dynamic-slice_bitcast_fusion.2
  108.1 1.3 multiply_exponential_fusion.2
  110.1 1.9 %multiply_add_fusion.3 = f32[2,4,256,128]{3,2,0,1:T(8,128)S(1)} fusion(f32[2,256,128]{2,1,0:T(8,128)} %get-tuple-element.271, f32[2,4]{0,1:T(4,128)S(1)} %copy.83, f32[2,256,128]{2,1,0:T(8,128)} %get-tuple-element.273, f32[2,4]{0,1:T(4,128)S(1)} %copy.84, f32[2,256,128]{2,1,0:T(8,128)} %get-tuple-element.275, f32[2,4]{0,1:T(4,128)S(1)} %copy.85, ...), kind=kLoop, calls=%fused_computation.4.clone.1 | loop fusion | flops 3932160 | bytes 3145984 | tf_op jit(solution)/shard_map/while/body/eval_jaxpr/add | solution.py:80
  112.0 1.7 %fusion.90 = (f32[2,256,128]{2,1,0:T(8,128)}, f32[2,256,128]{2,1,0:T(8,128)S(1)}, f32[2,256,128]{2,1,0:T(8,128)S(1)}) fusion(f32[2,4,256,128]{3,2,0,1:T(8,128)S(1)} %multiply_add_fusion.3, f32[2,256,128]{2,1,0:T(8,128)} %get-tuple-element.301, pred[]{:T(512)S(6)} %compare.5, f32[2,256,256]{2,1,0:T(8,128)S(1)} %bitcast.77), kind=kLoop, calls=%fused_computation.26.clone.1 | loop fusion | flops 393216 | bytes 1572865 | tf_op jit(solution)/shard_map/while/body/eval_jaxpr/mul | solution.py:85
  115.9 0.9 dynamic-slice_bitcast_fusion.2
  117.3 1.3 multiply_exponential_fusion.2
  119.3 1.9 %multiply_add_fusion.3 = f32[2,4,256,128]{3,2,0,1:T(8,128)S(1)} fusion(f32[2,256,128]{2,1,0:T(8,128)} %get-tuple-element.271, f32[2,4]{0,1:T(4,128)S(1)} %copy.83, f32[2,256,128]{2,1,0:T(8,128)} %get-tuple-element.273, f32[2,4]{0,1:T(4,128)S(1)} %copy.84, f32[2,256,128]{2,1,0:T(8,128)} %get-tuple-element.275, f32[2,4]{0,1:T(4,128)S(1)} %copy.85, ...), kind=kLoop, calls=%fused_computation.4.clone.1 | loop fusion | flops 3932160 | bytes 3145984 | tf_op jit(solution)/shard_map/while/body/eval_jaxpr/add | solution.py:80
  121.3 1.7 %fusion.90 = (f32[2,256,128]{2,1,0:T(8,128)}, f32[2,256,128]{2,1,0:T(8,128)S(1)}, f32[2,256,128]{2,1,0:T(8,128)S(1)}) fusion(f32[2,4,256,128]{3,2,0,1:T(8,128)S(1)} %multiply_add_fusion.3, f32[2,256,128]{2,1,0:T(8,128)} %get-tuple-element.301, pred[]{:T(512)S(6)} %compare.5, f32[2,256,256]{2,1,0:T(8,128)S(1)} %bitcast.77), kind=kLoop, calls=%fused_computation.26.clone.1 | loop fusion | flops 393216 | bytes 1572865 | tf_op jit(solution)/shard_map/while/body/eval_jaxpr/mul | solution.py:85
  125.1 0.9 dynamic-slice_bitcast_fusion.2
  126.5 1.3 multiply_exponential_fusion.2
  128.6 1.9 %multiply_add_fusion.3 = f32[2,4,256,128]{3,2,0,1:T(8,128)S(1)} fusion(f32[2,256,128]{2,1,0:T(8,128)} %get-tuple-element.271, f32[2,4]{0,1:T(4,128)S(1)} %copy.83, f32[2,256,128]{2,1,0:T(8,128)} %get-tuple-element.273, f32[2,4]{0,1:T(4,128)S(1)} %copy.84, f32[2,256,128]{2,1,0:T(8,128)} %get-tuple-element.275, f32[2,4]{0,1:T(4,128)S(1)} %copy.85, ...), kind=kLoop, calls=%fused_computation.4.clone.1 | loop fusion | flops 3932160 | bytes 3145984 | tf_op jit(solution)/shard_map/while/body/eval_jaxpr/add | solution.py:80
  130.5 1.7 %fusion.90 = (f32[2,256,128]{2,1,0:T(8,128)}, f32[2,256,128]{2,1,0:T(8,128)S(1)}, f32[2,256,128]{2,1,0:T(8,128)S(1)}) fusion(f32[2,4,256,128]{3,2,0,1:T(8,128)S(1)} %multiply_add_fusion.3, f32[2,256,128]{2,1,0:T(8,128)} %get-tuple-element.301, pred[]{:T(512)S(6)} %compare.5, f32[2,256,256]{2,1,0:T(8,128)S(1)} %bitcast.77), kind=kLoop, calls=%fused_computation.26.clone.1 | loop fusion | flops 393216 | bytes 1572865 | tf_op jit(solution)/shard_map/while/body/eval_jaxpr/mul | solution.py:85
  134.3 0.9 dynamic-slice_bitcast_fusion.2
  135.7 1.3 multiply_exponential_fusion.2
  137.8 1.9 %multiply_add_fusion.3 = f32[2,4,256,128]{3,2,0,1:T(8,128)S(1)} fusion(f32[2,256,128]{2,1,0:T(8,128)} %get-tuple-element.271, f32[2,4]{0,1:T(4,128)S(1)} %copy.83, f32[2,256,128]{2,1,0:T(8,128)} %get-tuple-element.273, f32[2,4]{0,1:T(4,128)S(1)} %copy.84, f32[2,256,128]{2,1,0:T(8,128)} %get-tuple-element.275, f32[2,4]{0,1:T(4,128)S(1)} %copy.85, ...), kind=kLoop, calls=%fused_computation.4.clone.1 | loop fusion | flops 3932160 | bytes 3145984 | tf_op jit(solution)/shard_map/while/body/eval_jaxpr/add | solution.py:80
  139.7 1.7 %fusion.90 = (f32[2,256,128]{2,1,0:T(8,128)}, f32[2,256,128]{2,1,0:T(8,128)S(1)}, f32[2,256,128]{2,1,0:T(8,128)S(1)}) fusion(f32[2,4,256,128]{3,2,0,1:T(8,128)S(1)} %multiply_add_fusion.3, f32[2,256,128]{2,1,0:T(8,128)} %get-tuple-element.301, pred[]{:T(512)S(6)} %compare.5, f32[2,256,256]{2,1,0:T(8,128)S(1)} %bitcast.77), kind=kLoop, calls=%fused_computation.26.clone.1 | loop fusion | flops 393216 | bytes 1572865 | tf_op jit(solution)/shard_map/while/body/eval_jaxpr/mul | solution.py:85
  143.1 19.1 %all_to_all.18 = bf16[1,2,4,256,128]{4,2,1,0,3:T(4,128)(2,1)S(1)} all-to-all(bf16[1,2,4,256,128]{4,2,1,0,3:T(4,128)(2,1)S(1)} %bitcast.78), channel_id=1, replica_groups=mesh['depth'=4,'tile'=8] {'depth'}, dimensions={3} | all-to-all | bytes 1048576 | tf_op jit(solution)/shard_map/all_to_all | solution.py:111
  163.5 1.4 multiply_reduce_fusion
  (177 shorter events, 30.6 us)
Async XLA Ops:
  1.3 14.7 %collective-permute-start = (bf16[8,256,128]{1,2,0:T(8,128)(2,1)S(1)}, bf16[8,256,128]{1,2,0:T(8,128)(2,1)S(1)}, u32[]{:S(2)}, u32[]{:S(2)}) collective-permute-start(bf16[8,256,128]{1,2,0:T(8,128)(2,1)S(1)} %copy.51), channel_id=1, source_target_pairs={{0,8},{8,16},{16,24},{1,9},{9,17},{17,25},{2,10},{10,18},{18,26},{... | collective-permute-start | bytes 1572872 | tf_op jit(solution)/shard_map/ppermute | solution.py:16
  4.8 15.3 %collective-permute-start.1 = (bf16[8,256,128]{1,2,0:T(8,128)(2,1)S(1)}, bf16[8,256,128]{1,2,0:T(8,128)(2,1)S(1)}, u32[]{:S(2)}, u32[]{:S(2)}) collective-permute-start(bf16[8,256,128]{1,2,0:T(8,128)(2,1)S(1)} %copy.51), channel_id=1, source_target_pairs={{8,0},{16,8},{24,16},{9,1},{17,9},{25,17},{10,2},{18,10},{26,18},{... | collective-permute-start | bytes 1572872 | tf_op jit(solution)/shard_map/ppermute | solution.py:19
  20.1 7.2 %collective-permute-start.2 = (bf16[24,256,8]{1,2,0:T(8,128)(2,1)S(1)}, bf16[24,256,8]{1,2,0:T(8,128)(2,1)S(1)}, u32[]{:S(2)}, u32[]{:S(2)}) collective-permute-start(bf16[24,256,8]{1,2,0:T(8,128)(2,1)S(1)} %get-tuple-element.190), channel_id=1, source_target_pairs={{0,1},{1,2},{2,3},{3,4},{4,5},{5,6},{6,7},{8,9},{9,10},{10,11},{11... | collective-permute-start | bytes 294920 | tf_op jit(solution)/shard_map/ppermute | solution.py:16
  22.0 6.7 %collective-permute-start.3 = (bf16[24,256,8]{1,2,0:T(8,128)(2,1)S(1)}, bf16[24,256,8]{1,2,0:T(8,128)(2,1)S(1)}, u32[]{:S(2)}, u32[]{:S(2)}) collective-permute-start(bf16[24,256,8]{1,2,0:T(8,128)(2,1)S(1)} %get-tuple-element.191), channel_id=1, source_target_pairs={{1,0},{2,1},{3,2},{4,3},{5,4},{6,5},{7,6},{9,8},{10,9},{11,10},{12... | collective-permute-start | bytes 294920 | tf_op jit(solution)/shard_map/ppermute | solution.py:19
  69.7 0.8 copy-start
  77.0 1.0 copy-start.1
  78.0 0.8 copy-start
  86.2 1.0 copy-start.1
  87.3 0.8 copy-start
  95.4 1.0 copy-start.1
  96.5 0.8 copy-start
  104.7 1.0 copy-start.1
  105.7 0.8 copy-start
  113.9 1.0 copy-start.1
  114.9 0.8 copy-start
  123.1 1.0 copy-start.1
  124.2 0.8 copy-start
  132.4 1.0 copy-start.1
  133.4 0.8 copy-start
  141.6 1.0 copy-start.1
  142.7 19.5 %copy-start.2 = (s32[2,4]{1,0:T(2,128)S(1)}, s32[2,4]{1,0:T(2,128)}, u32[]{:S(2)}) copy-start(s32[2,4]{1,0:T(2,128)} %param.11) | copy-start | bytes 100
where the time goes:
time: 167 us; the launch traced here: 165 us
  other arithmetic  87.5 us (52%)
  local copies, waits for them, and re-layouts  30 us (18%)
  blocking collectives  19.1 us (11%)
  waiting for transfers between devices  12.6 us (8%)
  starting transfers between devices  11.3 us (7%)
  matrix products  3.66 us (2%)
    all_to_all x1, blocking collectives, local(): lax.all_to_all(slab_rgba[None], 'depth', split_axis=3, concat_axis=0, til...  19.1 us
    add x1, other arithmetic, occlusion_of(): along_rows + tap_weights[tap_index] * padded_rows[:, tap_index:tap_index...  15.6 us
    add x8, other arithmetic, one_slice(): values + tf_weights[:, :, basis_index][:, :, None, None] * bump_value[:,...  15.3 us
    mul x8, other arithmetic, one_slice(): passing = passing * (1.0 - opacity)  13 us
    convert_element_type x1, other arithmetic, occlusion_of(): return jnp.exp(-OCCLUSION_GAIN * along_width).astype(jnp.bfloat16)  12.8 us
    add x1, other arithmetic, occlusion_of(): along_depth + tap_weights[tap_index] * padded[tap_index:tap_index + depth...  12.5 us
    while x32, local copies, waits for them, and re-layouts  11.6 us
    exp x8, other arithmetic, one_slice(): bump_value = jnp.exp(-0.5 * offset * offset)  10.5 us
  transfers between devices with their start and end apart: 4, of which 3 were waited for; matrix products, arithmetic and copies ran while one was open for 2% of the time, Pallas kernels for 0%

commit v1 on v0

--- a/solution.py
+++ b/solution.py
@@ -6,6 +6,13 @@
 RADIUS = 8
 OCCLUSION_GAIN = 1.5
 EXTINCTION = 0.5
+
+
+def stacked_exchange(block, axis, split, join):
+    peers = lax.axis_size(axis)
+    blocks = jnp.stack(jnp.split(block, peers, axis=split), axis=0)
+    blocks = lax.all_to_all(blocks, axis, split_axis=0, concat_axis=0)
+    return jnp.concatenate(blocks, axis=join)
 
 
 def with_halo(block, sides, width):
@@ -108,7 +115,7 @@
     ordered = jnp.einsum(
         "vqj,jvcrx->vqcrx",
         selector,
-        lax.all_to_all(slab_rgba[None], "depth", split_axis=3, concat_axis=0, tiled=True),
+        stacked_exchange(slab_rgba[None], "depth", 3, 0),
         preferred_element_type=jnp.float32,
     )
     running = jnp.cumprod(1.0 - ordered[:, :, 3], axis=1)

time: 167 us -> 162 us (0.970)
  local copies, waits for them, and re-layouts: 30 us -> 24.9 us
    while x32 -> x1, local copies, waits for them, and re-layouts: 11.6 us -> 0.08 us  [render_slab(): final_state, _ = lax.scan(one_slice, initial, (slab_density, slab_shade))]
    dynamic_slice x16, local copies, waits for them, and re-layouts: 0.93 us -> 7.67 us  [render_slab(): final_state, _ = lax.scan(one_slice, initial, (slab_density, slab_shade))]
where the time goes in v1:
time: 162 us; the launch traced here: 160 us
  other arithmetic  88 us (54%)
  local copies, waits for them, and re-layouts  24.9 us (15%)
  blocking collectives  19.1 us (12%)
  waiting for transfers between devices  12.6 us (8%)
  starting transfers between devices  11.3 us (7%)
  matrix products  3.43 us (2%)
    all_to_all x1, blocking collectives, stacked_exchange(): blocks = lax.all_to_all(blocks, axis, split_axis=0, concat_axis=0)  19.1 us
    add x1, other arithmetic, occlusion_of(): along_rows + tap_weights[tap_index] * padded_rows[:, tap_index:tap_index...  15.5 us
    add x8, other arithmetic, one_slice(): values + tf_weights[:, :, basis_index][:, :, None, None] * bump_value[:,...  15.3 us
    convert_element_type x1, other arithmetic, occlusion_of(): return jnp.exp(-OCCLUSION_GAIN * along_width).astype(jnp.bfloat16)  13.4 us
    mul x8, other arithmetic, one_slice(): passing = passing * (1.0 - opacity)  13 us
    add x1, other arithmetic, occlusion_of(): along_depth + tap_weights[tap_index] * padded[tap_index:tap_index + depth...  12.4 us
    exp x8, other arithmetic, one_slice(): bump_value = jnp.exp(-0.5 * offset * offset)  10.5 us
    dynamic_slice x16, local copies, waits for them, and re-layouts, render_slab(): final_state, _ = lax.scan(one_slice, initial, (slab_density, slab_shade))  7.67 us
  transfers between devices with their start and end apart: 4, of which 3 were waited for; matrix products, arithmetic and copies ran while one was open for 2% of the time, Pallas kernels for 0%

profile of v1, /device:TPU:4, one launch (start us, length us, event | category | flops | bytes accessed | tf_op | source)
XLA Modules:
  0.0 160.0 jit_solution(15390359243734307297)
XLA Ops:
  0.0 1.2 copy.96
  1.3 3.5 %collective-permute-start = (bf16[8,256,128]{1,2,0:T(8,128)(2,1)S(1)}, bf16[8,256,128]{1,2,0:T(8,128)(2,1)S(1)}, u32[]{:S(2)}, u32[]{:S(2)}) collective-permute-start(bf16[8,256,128]{1,2,0:T(8,128)(2,1)S(1)} %copy.96), channel_id=1, source_target_pairs={{0,8},{8,16},{16,24},{1,9},{9,17},{17,25},{2,10},{10,18},{18,26},{... | collective-permute-start | bytes 1572872 | tf_op jit(solution)/shard_map/ppermute | solution.py:23
  4.8 1.3 collective-permute-start.1
  8.9 7.0 %collective-permute-done = bf16[8,256,128]{1,2,0:T(8,128)(2,1)S(1)} collective-permute-done((bf16[8,256,128]{1,2,0:T(8,128)(2,1)S(1)}, bf16[8,256,128]{1,2,0:T(8,128)(2,1)S(1)}, u32[]{:S(2)}, u32[]{:S(2)}) %collective-permute-start) | collective-permute-done | bytes 524320 | tf_op jit(solution)/shard_map/ppermute | solution.py:23
  15.9 4.1 %collective-permute-done.1 = bf16[8,256,128]{1,2,0:T(8,128)(2,1)S(1)} collective-permute-done((bf16[8,256,128]{1,2,0:T(8,128)(2,1)S(1)}, bf16[8,256,128]{1,2,0:T(8,128)(2,1)S(1)}, u32[]{:S(2)}, u32[]{:S(2)}) %collective-permute-start.1) | collective-permute-done | bytes 524320 | tf_op jit(solution)/shard_map/ppermute | solution.py:26
  20.1 1.9 %collective-permute-start.2 = (bf16[24,256,8]{1,2,0:T(8,128)(2,1)S(1)}, bf16[24,256,8]{1,2,0:T(8,128)(2,1)S(1)}, u32[]{:S(2)}, u32[]{:S(2)}) collective-permute-start(bf16[24,256,8]{1,2,0:T(8,128)(2,1)S(1)} %get-tuple-element.211), channel_id=1, source_target_pairs={{0,1},{1,2},{2,3},{3,4},{4,5},{5,6},{6,7},{8,9},{9,10},{10,11},{11... | collective-permute-start | bytes 294920 | tf_op jit(solution)/shard_map/ppermute | solution.py:23
  22.0 4.5 %collective-permute-start.3 = (bf16[24,256,8]{1,2,0:T(8,128)(2,1)S(1)}, bf16[24,256,8]{1,2,0:T(8,128)(2,1)S(1)}, u32[]{:S(2)}, u32[]{:S(2)}) collective-permute-start(bf16[24,256,8]{1,2,0:T(8,128)(2,1)S(1)} %get-tuple-element.212), channel_id=1, source_target_pairs={{1,0},{2,1},{3,2},{4,3},{5,4},{6,5},{7,6},{9,8},{10,9},{11,10},{12... | collective-permute-start | bytes 294920 | tf_op jit(solution)/shard_map/ppermute | solution.py:26
  27.3 1.5 collective-permute-done.3
  28.9 12.4 %multiply_add_fusion.1 = f32[8,256,144]{1,2,0:T(8,128)S(1)} fusion(bf16[24,256,144]{1,2,0:T(8,128)(2,1)S(1)} %pad_maximum_fusion, f32[]{:T(128)} %bitcast.18, f32[]{:T(128)} %bitcast.17, f32[]{:T(128)} %bitcast.16, f32[]{:T(128)} %bitcast.15, f32[]{:T(128)} %bitcast.14, f32[]{:T(128)} %bitcast.13, f32[]{:T(128)} %bitcast.12, f32[]{:T(128)} %bitcast.11, ...), kind=kLoop, calls=%fused_computation.98 | loop fusion | flops 14745600 | bytes 11206724 | tf_op jit(solution)/shard_map/add | solution.py:43
  41.3 15.5 %fusion.38 = f32[8,256,144]{1,2,0:T(8,128)S(1)} fusion(f32[8,256,144]{1,2,0:T(8,128)S(1)} %multiply_add_fusion.1, f32[]{:T(128)} %bitcast.18, f32[]{:T(128)} %bitcast.17, f32[]{:T(128)} %bitcast.16, f32[]{:T(128)} %bitcast.15, f32[]{:T(128)} %bitcast.14, f32[]{:T(128)} %bitcast.13, f32[]{:T(128)} %bitcast.12, f32[]{:T(128)} %bitcast.11, f32[]{:T(128)} %bitcast.10, ...), kind=kLoop, calls=%fused_computation.82 | loop fusion | flops 9732096 | bytes 2359364 | tf_op jit(solution)/shard_map/add | solution.py:50
  56.8 13.4 %fusion.57 = bf16[8,256,128]{1,2,0:T(8,128)(2,1)} fusion(f32[8,256,144]{1,2,0:T(8,128)S(1)} %fusion.38, f32[]{:T(128)} %bitcast.18, f32[]{:T(128)} %bitcast.17, f32[]{:T(128)} %bitcast.16, f32[]{:T(128)} %bitcast.15, f32[]{:T(128)} %bitcast.14, f32[]{:T(128)} %bitcast.13, f32[]{:T(128)} %bitcast.12, f32[]{:T(128)} %bitcast.11, f32[]{:T(128)} %bitcast.10, ...), kind=kLoop, calls=%fused_computation.103 | loop fusion | flops 9175040 | bytes 18350148 | tf_op jit(solution)/shard_map/convert_element_type | solution.py:58
  70.2 68.1 %while.15 = (s32[]{:T(128)}, f32[2,4,256,128]{3,2,0,1:T(8,128)S(1)}, f32[2,256,128]{2,1,0:T(8,128)}, f32[2,4,8]{1,0,2:T(2,128)S(1)}, bf16[8,256,128]{2,1,0:T(8,1...) while((s32[]{:T(128)}, ...), condition=%wide.region_2.3_spmd.clone, body=%wide.region_1.2_spmd.clone.sunk | while | flops 75300864 | bytes 14945648 | solution.py:99
  71.1 0.9 dynamic-slice_bitcast_fusion.2
  72.5 1.3 multiply_exponential_fusion.2
  74.6 1.9 %multiply_add_fusion.3 = f32[2,4,256,128]{3,2,0,1:T(8,128)S(1)} fusion(f32[2,256,128]{2,1,0:T(8,128)} %get-tuple-element.296, f32[2,4]{0,1:T(4,128)S(1)} %copy.126, f32[2,256,128]{2,1,0:T(8,128)} %get-tuple-element.298, f32[2,4]{0,1:T(4,128)S(1)} %copy.127, f32[2,256,128]{2,1,0:T(8,128)} %get-tuple-element.300, f32[2,4]{0,1:T(4,128)S(1)} %copy.128, ...), kind=kLoop, calls=%fused_computation.4.clone.1 | loop fusion | flops 3932160 | bytes 3145984 | tf_op jit(solution)/shard_map/while/body/eval_jaxpr/add | solution.py:87
  77.8 0.8 constant_dynamic-slice_fusion.2
  78.8 0.9 dynamic-slice_bitcast_fusion.2
  80.2 1.3 multiply_exponential_fusion.2
  82.3 1.9 %multiply_add_fusion.3 = f32[2,4,256,128]{3,2,0,1:T(8,128)S(1)} fusion(f32[2,256,128]{2,1,0:T(8,128)} %get-tuple-element.296, f32[2,4]{0,1:T(4,128)S(1)} %copy.126, f32[2,256,128]{2,1,0:T(8,128)} %get-tuple-element.298, f32[2,4]{0,1:T(4,128)S(1)} %copy.127, f32[2,256,128]{2,1,0:T(8,128)} %get-tuple-element.300, f32[2,4]{0,1:T(4,128)S(1)} %copy.128, ...), kind=kLoop, calls=%fused_computation.4.clone.1 | loop fusion | flops 3932160 | bytes 3145984 | tf_op jit(solution)/shard_map/while/body/eval_jaxpr/add | solution.py:87
  84.2 1.7 %fusion.91 = (f32[2,256,128]{2,1,0:T(8,128)}, f32[2,256,128]{2,1,0:T(8,128)S(1)}, f32[2,256,128]{2,1,0:T(8,128)S(1)}) fusion(f32[2,4,256,128]{3,2,0,1:T(8,128)S(1)} %multiply_add_fusion.3, f32[2,256,128]{2,1,0:T(8,128)} %get-tuple-element.326, pred[]{:T(512)S(6)} %compare.5, f32[2,256,256]{2,1,0:T(8,128)S(1)} %bitcast.82), kind=kLoop, calls=%fused_computation.26.clone.1 | loop fusion | flops 393216 | bytes 1572865 | tf_op jit(solution)/shard_map/while/body/eval_jaxpr/mul | solution.py:92
  86.5 0.8 constant_dynamic-slice_fusion.2
  87.4 0.9 dynamic-slice_bitcast_fusion.2
  88.8 1.3 multiply_exponential_fusion.2
  90.9 1.9 %multiply_add_fusion.3 = f32[2,4,256,128]{3,2,0,1:T(8,128)S(1)} fusion(f32[2,256,128]{2,1,0:T(8,128)} %get-tuple-element.296, f32[2,4]{0,1:T(4,128)S(1)} %copy.126, f32[2,256,128]{2,1,0:T(8,128)} %get-tuple-element.298, f32[2,4]{0,1:T(4,128)S(1)} %copy.127, f32[2,256,128]{2,1,0:T(8,128)} %get-tuple-element.300, f32[2,4]{0,1:T(4,128)S(1)} %copy.128, ...), kind=kLoop, calls=%fused_computation.4.clone.1 | loop fusion | flops 3932160 | bytes 3145984 | tf_op jit(solution)/shard_map/while/body/eval_jaxpr/add | solution.py:87
  92.8 1.7 %fusion.91 = (f32[2,256,128]{2,1,0:T(8,128)}, f32[2,256,128]{2,1,0:T(8,128)S(1)}, f32[2,256,128]{2,1,0:T(8,128)S(1)}) fusion(f32[2,4,256,128]{3,2,0,1:T(8,128)S(1)} %multiply_add_fusion.3, f32[2,256,128]{2,1,0:T(8,128)} %get-tuple-element.326, pred[]{:T(512)S(6)} %compare.5, f32[2,256,256]{2,1,0:T(8,128)S(1)} %bitcast.82), kind=kLoop, calls=%fused_computation.26.clone.1 | loop fusion | flops 393216 | bytes 1572865 | tf_op jit(solution)/shard_map/while/body/eval_jaxpr/mul | solution.py:92
  95.1 0.8 constant_dynamic-slice_fusion.2
  96.1 0.9 dynamic-slice_bitcast_fusion.2
  97.5 1.3 multiply_exponential_fusion.2
  99.5 1.9 %multiply_add_fusion.3 = f32[2,4,256,128]{3,2,0,1:T(8,128)S(1)} fusion(f32[2,256,128]{2,1,0:T(8,128)} %get-tuple-element.296, f32[2,4]{0,1:T(4,128)S(1)} %copy.126, f32[2,256,128]{2,1,0:T(8,128)} %get-tuple-element.298, f32[2,4]{0,1:T(4,128)S(1)} %copy.127, f32[2,256,128]{2,1,0:T(8,128)} %get-tuple-element.300, f32[2,4]{0,1:T(4,128)S(1)} %copy.128, ...), kind=kLoop, calls=%fused_computation.4.clone.1 | loop fusion | flops 3932160 | bytes 3145984 | tf_op jit(solution)/shard_map/while/body/eval_jaxpr/add | solution.py:87
  101.5 1.7 %fusion.91 = (f32[2,256,128]{2,1,0:T(8,128)}, f32[2,256,128]{2,1,0:T(8,128)S(1)}, f32[2,256,128]{2,1,0:T(8,128)S(1)}) fusion(f32[2,4,256,128]{3,2,0,1:T(8,128)S(1)} %multiply_add_fusion.3, f32[2,256,128]{2,1,0:T(8,128)} %get-tuple-element.326, pred[]{:T(512)S(6)} %compare.5, f32[2,256,256]{2,1,0:T(8,128)S(1)} %bitcast.82), kind=kLoop, calls=%fused_computation.26.clone.1 | loop fusion | flops 393216 | bytes 1572865 | tf_op jit(solution)/shard_map/while/body/eval_jaxpr/mul | solution.py:92
  104.7 0.9 dynamic-slice_bitcast_fusion.2
  106.1 1.3 multiply_exponential_fusion.2
  108.2 1.9 %multiply_add_fusion.3 = f32[2,4,256,128]{3,2,0,1:T(8,128)S(1)} fusion(f32[2,256,128]{2,1,0:T(8,128)} %get-tuple-element.296, f32[2,4]{0,1:T(4,128)S(1)} %copy.126, f32[2,256,128]{2,1,0:T(8,128)} %get-tuple-element.298, f32[2,4]{0,1:T(4,128)S(1)} %copy.127, f32[2,256,128]{2,1,0:T(8,128)} %get-tuple-element.300, f32[2,4]{0,1:T(4,128)S(1)} %copy.128, ...), kind=kLoop, calls=%fused_computation.4.clone.1 | loop fusion | flops 3932160 | bytes 3145984 | tf_op jit(solution)/shard_map/while/body/eval_jaxpr/add | solution.py:87
  110.1 1.7 %fusion.91 = (f32[2,256,128]{2,1,0:T(8,128)}, f32[2,256,128]{2,1,0:T(8,128)S(1)}, f32[2,256,128]{2,1,0:T(8,128)S(1)}) fusion(f32[2,4,256,128]{3,2,0,1:T(8,128)S(1)} %multiply_add_fusion.3, f32[2,256,128]{2,1,0:T(8,128)} %get-tuple-element.326, pred[]{:T(512)S(6)} %compare.5, f32[2,256,256]{2,1,0:T(8,128)S(1)} %bitcast.82), kind=kLoop, calls=%fused_computation.26.clone.1 | loop fusion | flops 393216 | bytes 1572865 | tf_op jit(solution)/shard_map/while/body/eval_jaxpr/mul | solution.py:92
  113.3 0.9 dynamic-slice_bitcast_fusion.2
  114.7 1.3 multiply_exponential_fusion.2
  116.8 1.9 %multiply_add_fusion.3 = f32[2,4,256,128]{3,2,0,1:T(8,128)S(1)} fusion(f32[2,256,128]{2,1,0:T(8,128)} %get-tuple-element.296, f32[2,4]{0,1:T(4,128)S(1)} %copy.126, f32[2,256,128]{2,1,0:T(8,128)} %get-tuple-element.298, f32[2,4]{0,1:T(4,128)S(1)} %copy.127, f32[2,256,128]{2,1,0:T(8,128)} %get-tuple-element.300, f32[2,4]{0,1:T(4,128)S(1)} %copy.128, ...), kind=kLoop, calls=%fused_computation.4.clone.1 | loop fusion | flops 3932160 | bytes 3145984 | tf_op jit(solution)/shard_map/while/body/eval_jaxpr/add | solution.py:87
  118.7 1.7 %fusion.91 = (f32[2,256,128]{2,1,0:T(8,128)}, f32[2,256,128]{2,1,0:T(8,128)S(1)}, f32[2,256,128]{2,1,0:T(8,128)S(1)}) fusion(f32[2,4,256,128]{3,2,0,1:T(8,128)S(1)} %multiply_add_fusion.3, f32[2,256,128]{2,1,0:T(8,128)} %get-tuple-element.326, pred[]{:T(512)S(6)} %compare.5, f32[2,256,256]{2,1,0:T(8,128)S(1)} %bitcast.82), kind=kLoop, calls=%fused_computation.26.clone.1 | loop fusion | flops 393216 | bytes 1572865 | tf_op jit(solution)/shard_map/while/body/eval_jaxpr/mul | solution.py:92
  121.9 0.9 dynamic-slice_bitcast_fusion.2
  123.4 1.3 multiply_exponential_fusion.2
  125.4 1.9 %multiply_add_fusion.3 = f32[2,4,256,128]{3,2,0,1:T(8,128)S(1)} fusion(f32[2,256,128]{2,1,0:T(8,128)} %get-tuple-element.296, f32[2,4]{0,1:T(4,128)S(1)} %copy.126, f32[2,256,128]{2,1,0:T(8,128)} %get-tuple-element.298, f32[2,4]{0,1:T(4,128)S(1)} %copy.127, f32[2,256,128]{2,1,0:T(8,128)} %get-tuple-element.300, f32[2,4]{0,1:T(4,128)S(1)} %copy.128, ...), kind=kLoop, calls=%fused_computation.4.clone.1 | loop fusion | flops 3932160 | bytes 3145984 | tf_op jit(solution)/shard_map/while/body/eval_jaxpr/add | solution.py:87
  127.3 1.7 %fusion.91 = (f32[2,256,128]{2,1,0:T(8,128)}, f32[2,256,128]{2,1,0:T(8,128)S(1)}, f32[2,256,128]{2,1,0:T(8,128)S(1)}) fusion(f32[2,4,256,128]{3,2,0,1:T(8,128)S(1)} %multiply_add_fusion.3, f32[2,256,128]{2,1,0:T(8,128)} %get-tuple-element.326, pred[]{:T(512)S(6)} %compare.5, f32[2,256,256]{2,1,0:T(8,128)S(1)} %bitcast.82), kind=kLoop, calls=%fused_computation.26.clone.1 | loop fusion | flops 393216 | bytes 1572865 | tf_op jit(solution)/shard_map/while/body/eval_jaxpr/mul | solution.py:92
  130.6 0.9 dynamic-slice_bitcast_fusion.2
  132.0 1.3 multiply_exponential_fusion.2
  134.0 1.9 %multiply_add_fusion.3 = f32[2,4,256,128]{3,2,0,1:T(8,128)S(1)} fusion(f32[2,256,128]{2,1,0:T(8,128)} %get-tuple-element.296, f32[2,4]{0,1:T(4,128)S(1)} %copy.126, f32[2,256,128]{2,1,0:T(8,128)} %get-tuple-element.298, f32[2,4]{0,1:T(4,128)S(1)} %copy.127, f32[2,256,128]{2,1,0:T(8,128)} %get-tuple-element.300, f32[2,4]{0,1:T(4,128)S(1)} %copy.128, ...), kind=kLoop, calls=%fused_computation.4.clone.1 | loop fusion | flops 3932160 | bytes 3145984 | tf_op jit(solution)/shard_map/while/body/eval_jaxpr/add | solution.py:87
  136.0 1.7 %fusion.91 = (f32[2,256,128]{2,1,0:T(8,128)}, f32[2,256,128]{2,1,0:T(8,128)S(1)}, f32[2,256,128]{2,1,0:T(8,128)S(1)}) fusion(f32[2,4,256,128]{3,2,0,1:T(8,128)S(1)} %multiply_add_fusion.3, f32[2,256,128]{2,1,0:T(8,128)} %get-tuple-element.326, pred[]{:T(512)S(6)} %compare.5, f32[2,256,256]{2,1,0:T(8,128)S(1)} %bitcast.82), kind=kLoop, calls=%fused_computation.26.clone.1 | loop fusion | flops 393216 | bytes 1572865 | tf_op jit(solution)/shard_map/while/body/eval_jaxpr/mul | solution.py:92
  138.4 19.1 %all_to_all.5 = bf16[4,1,2,4,64,128]{5,4,3,2,1,0:T(8,128)(2,1)S(1)} all-to-all(bf16[4,1,2,4,64,128]{5,4,3,2,1,0:T(8,128)(2,1)S(1)} %pad_maximum_fusion.1), channel_id=1, replica_groups=mesh['depth'=4,'tile'=8] {'depth'}, dimensions={0} | all-to-all | bytes 1048576 | tf_op jit(solution)/shard_map/all_to_all | solution.py:14
  158.6 1.4 multiply_reduce_fusion
  (146 shorter events, 25.0 us)
Async XLA Ops:
  1.3 14.7 %collective-permute-start = (bf16[8,256,128]{1,2,0:T(8,128)(2,1)S(1)}, bf16[8,256,128]{1,2,0:T(8,128)(2,1)S(1)}, u32[]{:S(2)}, u32[]{:S(2)}) collective-permute-start(bf16[8,256,128]{1,2,0:T(8,128)(2,1)S(1)} %copy.96), channel_id=1, source_target_pairs={{0,8},{8,16},{16,24},{1,9},{9,17},{17,25},{2,10},{10,18},{18,26},{... | collective-permute-start | bytes 1572872 | tf_op jit(solution)/shard_map/ppermute | solution.py:23
  4.8 15.3 %collective-permute-start.1 = (bf16[8,256,128]{1,2,0:T(8,128)(2,1)S(1)}, bf16[8,256,128]{1,2,0:T(8,128)(2,1)S(1)}, u32[]{:S(2)}, u32[]{:S(2)}) collective-permute-start(bf16[8,256,128]{1,2,0:T(8,128)(2,1)S(1)} %copy.96), channel_id=1, source_target_pairs={{8,0},{16,8},{24,16},{9,1},{17,9},{25,17},{10,2},{18,10},{26,18},{... | collective-permute-start | bytes 1572872 | tf_op jit(solution)/shard_map/ppermute | solution.py:26
  20.1 7.2 %collective-permute-start.2 = (bf16[24,256,8]{1,2,0:T(8,128)(2,1)S(1)}, bf16[24,256,8]{1,2,0:T(8,128)(2,1)S(1)}, u32[]{:S(2)}, u32[]{:S(2)}) collective-permute-start(bf16[24,256,8]{1,2,0:T(8,128)(2,1)S(1)} %get-tuple-element.211), channel_id=1, source_target_pairs={{0,1},{1,2},{2,3},{3,4},{4,5},{5,6},{6,7},{8,9},{9,10},{10,11},{11... | collective-permute-start | bytes 294920 | tf_op jit(solution)/shard_map/ppermute | solution.py:23
  22.0 6.7 %collective-permute-start.3 = (bf16[24,256,8]{1,2,0:T(8,128)(2,1)S(1)}, bf16[24,256,8]{1,2,0:T(8,128)(2,1)S(1)}, u32[]{:S(2)}, u32[]{:S(2)}) collective-permute-start(bf16[24,256,8]{1,2,0:T(8,128)(2,1)S(1)} %get-tuple-element.212), channel_id=1, source_target_pairs={{1,0},{2,1},{3,2},{4,3},{5,4},{6,5},{7,6},{9,8},{10,9},{11,10},{12... | collective-permute-start | bytes 294920 | tf_op jit(solution)/shard_map/ppermute | solution.py:26
  138.3 19.2 %copy-start = (s32[2,4]{1,0:T(2,128)S(1)}, s32[2,4]{1,0:T(2,128)}, u32[]{:S(2)}) copy-start(s32[2,4]{1,0:T(2,128)} %param.11) | copy-start | bytes 100
